TPU v7x, 512 devices: a whole 4x8x8 slice. The times are simulated.
512 devices in a mesh: tgt: 64 (over z, y_hi, core), sup: 8 (over x, y_lo).
Axes of the slice: x: 4, y: 8 (y_hi: 4, y_lo: 2; y = y_hi * 2 + y_lo), z: 8, core: 2. Of those that a mesh axis runs over, the one named last changes fastest.
Arguments:
- targets: float32 [512, 3, 1024], P('tgt'), may hold values from -4 to 4
- labels: int32 [512], P('tgt'), may hold values from 0 to 99
- support_slots: float32 [64, 64, 3, 1024], P('tgt', 'sup'), may hold values from -4 to 4
- block_owner: int32 [4], replicated, may hold values from 0 to 63, as said below
- dual_coeffs: float32 [4, 64, 100], P(None, 'sup'), may hold values from -0.15 to 0.15
Outputs:
- predictions: float32 [512, 100], P('tgt')
- support_grad: float32 [4, 64, 3, 1024], P(None, 'sup')
Inputs may be any that keep to these rules, and one draw needn't show every extreme that they name: 4 distinct slot indices, among them 0 and 63; block b is support_slots[block_owner[b]], and the other slots are never read.
All inputs are finite; a program needn't handle non-finite values.
Results may differ from a plain program's by a relative error of at most 0.0001.
Values sent between devices are 32-bit elements; how exact they have to be, the bound alone decides.
No kernel may reach another device: no remote copies, remote signals or barrier semaphores. Data moves between devices by JAX's collectives and lax.ppermute only.
A program may use at most 64 MiB of HBM per device.

v0:
```python
import jax
import jax.numpy as jnp
from jax import lax
from jax.sharding import PartitionSpec as P

SIDE = 32
LAYERS = 3
weight_variance = 1.6
bias_variance = 0.1
loss_weight = 64.0
arcsin_scale = 2.0 / 3.141592653589793


def broadcast(array, axis, root):
    mine = lax.axis_index(axis) == root
    return lax.psum(jnp.where(mine, array, jnp.zeros_like(array)), axis)


def box_sum(states, grid_side):
    length = states.shape[-1]
    column = lax.broadcasted_iota(jnp.int32, (length,), 0) % grid_side
    zero_column = jnp.zeros(states.shape[:-1] + (1,), states.dtype)
    from_left = jnp.where(
        column > 0, jnp.concatenate([zero_column, states[..., :-1]], axis=-1), 0.0
    )
    from_right = jnp.where(
        column < grid_side - 1, jnp.concatenate([states[..., 1:], zero_column], axis=-1), 0.0
    )
    row_sum = states + from_left + from_right
    zero_row = jnp.zeros(states.shape[:-1] + (grid_side,), states.dtype)
    from_above = jnp.concatenate([zero_row, row_sum[..., :-grid_side]], axis=-1)
    from_below = jnp.concatenate([row_sum[..., grid_side:], zero_row], axis=-1)
    return row_sum + from_above + from_below


def self_chain(images):
    squares = images[:, 0, :] * images[:, 0, :]
    for channel in range(1, images.shape[1]):
        squares = squares + images[:, channel, :] * images[:, channel, :]
    variance = weight_variance * box_sum(squares / images.shape[1], SIDE) / 9.0 + bias_variance
    variances = [variance]
    for layer_index in range(1, LAYERS):
        activated = arcsin_scale * jnp.arcsin(2.0 * variance / (1.0 + 2.0 * variance))
        variance = weight_variance * box_sum(activated, SIDE) / 9.0 + bias_variance
        variances.append(variance)
    return variances


def pair_kernel(support, support_variances, targets, target_variances):
    cross_terms = targets[:, 0, :][:, None, :] * support[:, 0, :][None, :, :]
    for channel in range(1, support.shape[1]):
        cross_terms = (
            cross_terms + targets[:, channel, :][:, None, :] * support[:, channel, :][None, :, :]
        )
    preact = weight_variance * box_sum(cross_terms / support.shape[1], SIDE) / 9.0 + bias_variance
    tangent = preact
    activated = preact
    slope = preact
    for layer_index in range(LAYERS):
        product = (1.0 + 2.0 * target_variances[layer_index])[:, None, :] * (
            1.0 + 2.0 * support_variances[layer_index]
        )[None, :, :]
        activated = arcsin_scale * jnp.arcsin(2.0 * preact / jnp.sqrt(product))
        slope = 2.0 * arcsin_scale / jnp.sqrt(product - 4.0 * preact * preact)
        if layer_index + 1 < LAYERS:
            preact_next = weight_variance * box_sum(activated, SIDE) / 9.0 + bias_variance
            tangent = preact_next + weight_variance * box_sum(tangent * slope, SIDE) / 9.0
            preact = preact_next
    return jnp.mean(weight_variance * (activated + tangent * slope) + bias_variance, axis=-1)


def sum_states(images_part, variance_part):
    return lax.psum((images_part, variance_part), "tgt")


def local(targets, labels, support_slots, block_owner, dual_coeffs):
    own_slot = support_slots[0]
    target_variances = self_chain(targets)
    block_count = dual_coeffs.shape[0]
    classes = dual_coeffs.shape[-1]

    def kernel_rows_of(images, variances):
        return pair_kernel(images, variances, targets, target_variances)

    partial_value = jnp.zeros((targets.shape[0], classes), jnp.float32)
    supports = []
    support_sets = []
    self_pullbacks = []
    pullbacks = []
    for block_index in range(block_count):
        support = broadcast(own_slot, "tgt", block_owner[block_index])
        support_variances, self_pullback = jax.vjp(self_chain, support)
        kernel, pullback = jax.vjp(kernel_rows_of, support, support_variances)
        pullbacks.append(pullback)
        supports.append(support)
        support_sets.append(support_variances)
        self_pullbacks.append(self_pullback)
        partial_value = partial_value + jnp.dot(
            kernel, dual_coeffs[block_index], precision=lax.Precision.HIGHEST
        )
    predictions = lax.psum(partial_value, "sup")
    onehot = (labels[:, None] == lax.broadcasted_iota(jnp.int32, (1, classes), 1)).astype(
        jnp.float32
    )
    residual_error = loss_weight * (predictions - onehot)
    image_terms = []
    variance_terms = []
    for block_index in range(block_count):
        pair_weights = jnp.dot(
            residual_error, dual_coeffs[block_index].T, precision=lax.Precision.HIGHEST
        )
        grad_images, grad_variances = pullbacks[block_index](pair_weights)
        image_terms.append(grad_images)
        variance_terms.append(jnp.stack(grad_variances))
    gradients = []
    for block_index in range(block_count):
        summed_images, summed_variances = sum_states(
            image_terms[block_index], variance_terms[block_index]
        )
        variance_list = [summed_variances[layer_index] for layer_index in range(LAYERS)]
        gradients.append(summed_images + self_pullbacks[block_index](variance_list)[0])
    return (predictions, jnp.stack(gradients))


def solution(mesh):
    return jax.shard_map(
        local,
        mesh=mesh,
        in_specs=(
            P("tgt", None, None),
            P("tgt"),
            P("tgt", "sup", None, None),
            P(),
            P(None, "sup", None),
        ),
        out_specs=(P("tgt", None), P(None, "sup", None, None)),
        check_vma=False,
    )
```

profile of v0, /device:TPU:1, one launch (start us, length us, event | category | flops | bytes accessed | tf_op | source)
XLA Modules:
  0.0 1204.3 jit_solution(16650220429389493855)
XLA Ops:
  7.9 0.7 fusion.412
  11.2 1.6 select_bitcast_fusion.3
  13.0 0.7 copy-done.33
  14.4 545.0 %all-reduce.299.cloned.1.call-done = (f32[8,3,1024]{2,0,1:T(8,128)}, f32[8,3,1024]{2,0,1:T(8,128)}, f32[8,3,1024]{2,0,1:T(8,128)}, f32[8,3,1024]{2,0,1:T(8,128)}) async-done(((f32[8,3,1024]{2,0,1:T(8,128)}, f32[8,3,1024]{2,0,1:T(8,128)}, f32[8,3,1024]{2,0,1:T(8,128)}, f32[8,3,1024]{2,0,1:T(8,128)}), (f32[8,3,1024]{2,0,1:T(8,128)}, f32[8,3,1024]{2,0,1:T(8,128)}, f32[8,3,1024]{2,0,1:T(8,128)}, ...) | async-done | bytes 393232 | tf_op jit(solution)/shard_map/psum | solution.py:16
  559.4 0.9 add_multiply_fusion.34
  560.4 0.9 copy-done.7
  571.4 1.4 fusion.227
  573.2 1.2 add_multiply_fusion.15
  578.1 2.1 add_multiply_fusion.1
  581.3 1.2 add_multiply_fusion.13
  584.9 4.2 add_reduce_fusion
  589.7 15.0 %psum.95 = f32[8,100]{1,0:T(8,128)S(1)} all-reduce(f32[8,100]{1,0:T(8,128)S(1)} %convolution_add_fusion), channel_id=1, replica_groups=mesh['tgt'=64,'sup'=8] {'sup'}, use_global_device_ids=true, to_apply=%region_8.9 | all-reduce | flops 800 | bytes 6400 | tf_op jit(solution)/shard_map/psum | solution.py:101
  604.8 0.9 broadcast_multiply_fusion.13
  605.7 0.9 broadcast_multiply_fusion.12
  606.6 0.9 broadcast_multiply_fusion.11
  607.6 0.9 broadcast_multiply_fusion.14
  608.5 2.8 fusion.206
  612.2 0.8 copy-done.1
  615.0 0.9 slice_select_fusion.15
  615.9 0.9 fusion.205
  616.8 0.9 fusion.211
  617.7 0.9 fusion.155
  620.5 1.0 fusion.204
  621.5 1.0 fusion.146
  622.5 0.9 fusion.125
  626.0 0.9 fusion.207
  626.9 1.0 fusion.116
  634.6 542.6 %all-reduce.297.cloned.1.call-done = (f32[8,3,1024]{2,0,1:T(8,128)}, f32[3,8,1024]{2,1,0:T(8,128)}, f32[8,3,1024]{2,0,1:T(8,128)}, f32[3,8,1024]{2,1,0:T(8,128)}...) async-done(((f32[8,3,1024]{2,0,1:T(8,128)}, f32[3,8,1024]{2,1,0:T(8,128)}, f32[8,3,1024]{2,0,1:T(8,128)}, ...) | async-done | bytes 786448 | tf_op jit(solution)/shard_map/psum | solution.py:73
  1177.3 0.8 fusion.240
  1178.1 0.8 fusion.247
  1179.4 0.7 copy-done.40
  1180.3 0.7 copy-done.46
  1181.1 0.8 copy-done.50
  1183.3 0.7 copy-done.28
  1184.1 0.7 copy-done.32
  1185.0 0.7 copy-done.30
  1185.8 0.8 copy-done.47
  1187.1 0.8 copy-done.10
  1188.0 0.9 copy-done.8
  1188.9 0.9 copy-done.6
  1189.9 0.7 copy-done.42
  1191.0 0.7 copy-done.26
  1192.0 0.8 copy-done.4
  1192.9 0.9 copy-done.57
  1193.8 0.9 copy-done.56
  1194.7 0.9 copy-done.55
  1195.6 0.9 copy-done.54
  1196.5 0.8 pad_maximum_fusion
  (339 shorter events, 37.3 us)
Async XLA Ops:
  7.2 552.2 %all-reduce.299.cloned.1.call-start = ((), (), s32[]{:S(2)}) async-start(), calls=%async_computation.1 | async-start | bytes 786432 | tf_op jit(solution)/shard_map/psum | solution.py:16
  12.8 0.9 copy-start.33
  12.8 1164.4 %all-reduce.297.cloned.1.call-start = ((), (), s32[]{:S(2)}) async-start(), calls=%async_computation | async-start | bytes 1572864 | tf_op jit(solution)/shard_map/psum | solution.py:73
  559.4 1.0 copy-start.3
  559.4 1.0 copy-start.5
  560.4 0.9 copy-start.7
  560.4 0.9 copy-start.9
  562.0 11.2 copy-start.17
  563.7 17.7 %copy-start.21 = (f32[8,1024]{1,0:T(8,128)}, f32[8,1024]{1,0:T(8,128)S(1)}, u32[]{:S(2)}) copy-start(f32[8,1024]{1,0:T(8,128)S(1)} %get-tuple-element.409) | copy-start | bytes 98308
  564.3 9.0 copy-start.15
  565.2 0.8 copy-start.39
  566.7 14.6 %copy-start.19 = (f32[8,1024]{1,0:T(8,128)}, f32[8,1024]{1,0:T(8,128)S(1)}, u32[]{:S(2)}) copy-start(f32[8,1024]{1,0:T(8,128)S(1)} %get-tuple-element.407) | copy-start | bytes 98308
  567.8 10.3 copy-start.13
  568.9 9.2 copy-start.11
  584.4 4.7 copy-start.37
  584.9 4.2 copy-start.58
  604.8 2.8 copy-start.60
  604.8 3.7 copy-start
  612.0 1.0 copy-start.1
  612.0 1.0 copy-start.2
  612.0 1.0 copy-start.24
  612.0 1.0 copy-start.38
  614.9 0.9 copy-start.20
  615.0 0.9 copy-start.22
  615.9 0.9 copy-start.12
  615.9 0.9 copy-start.14
  619.8 0.8 copy-start.18
  625.2 0.8 copy-start.16
  630.8 0.8 copy-start.52
  630.8 0.8 copy-start.53
  1177.3 1.6 copy-start.48
  1177.3 1.6 copy-start.49
  1179.3 0.8 copy-start.40
  1180.2 0.8 copy-start.46
  1181.0 0.9 copy-start.50
  1182.2 0.8 copy-start.44
  1183.2 0.8 copy-start.28
  1184.0 0.8 copy-start.32
  1185.7 0.9 copy-start.47
  1187.0 0.9 copy-start.10
  1187.9 0.9 copy-start.8
  1188.9 0.9 copy-start.6
  1190.9 0.8 copy-start.26
  1191.9 0.9 copy-start.4
  1192.9 0.9 copy-start.57
  1193.8 0.9 copy-start.56
  1194.7 0.9 copy-start.55
  1195.6 0.9 copy-start.54
  (15 other events, 9.6 us)
Sparse Core Ops, SparseCore 0:
  12.9 546.3 all-reduce.298
  634.8 542.4 all-reduce.296
where the time goes:
time: 1210 us; the launch traced here: 1200 us
  waiting for transfers between devices  1090 us (90%)
  other arithmetic  46 us (4%)
  local copies, waits for them, and re-layouts  33.1 us (3%)
  between operations  18.3 us (2%)
  blocking collectives  15 us (1%)
    psum x1, waiting for transfers between devices, broadcast(): return lax.psum(jnp.where(mine, array, jnp.zeros_like(array)), axis)  545 us
    psum x1, waiting for transfers between devices, sum_states(): return lax.psum((images_part, variance_part), 'tgt')  543 us
  transfers between devices with their start and end apart: 2, of which 2 were waited for; matrix products, arithmetic and copies ran while one was open for 0% of the time, Pallas kernels for 0%

commit v1 on v0

--- a/solution.py
+++ b/solution.py
@@ -13,7 +13,12 @@
 
 def broadcast(array, axis, root):
     mine = lax.axis_index(axis) == root
-    return lax.psum(jnp.where(mine, array, jnp.zeros_like(array)), axis)
+
+    def _take_roads(z_in):
+        u_next = jax.lax.all_gather(z_in, axis)
+        return jnp.sum(u_next, 0)
+
+    return _take_roads(jnp.where(mine, array, jnp.zeros_like(array)))
 
 
 def box_sum(states, grid_side):

time: 1210 us -> 1040 us (0.86)
  waiting for transfers between devices: 1090 us -> 910 us
  other arithmetic: 46 us -> 67.5 us
  local copies, waits for them, and re-layouts: 33.1 us -> 14.3 us
    psum x1 -> x0, waiting for transfers between devices: 545 us -> none  [broadcast(): return lax.psum(jnp.where(mine, array, jnp.zeros_like(array)), axis)]
    all_gather x0 -> x4, waiting for transfers between devices: none -> 368 us  [_take_roads(): u_next = jax.lax.all_gather(z_in, axis)]
    unnamed x122 -> x110, local copies, waits for them, and re-layouts: 21 us -> 0.23 us
    reduce_sum x0 -> x4, other arithmetic: none -> 12.5 us  [_take_roads(): return jnp.sum(u_next, 0)]
  transfers between devices with their start and end apart: 2 -> 5, of which waited for: 2 -> 5; matrix products, arithmetic and copies ran while one was open for 0% -> 1% of each run, Pallas kernels for 0% -> 0%
where the time goes in v1:
time: 1040 us; the launch traced here: 1030 us
  waiting for transfers between devices  910 us (88%)
  other arithmetic  67.5 us (6%)
  between operations  18.3 us (2%)
  blocking collectives  14.4 us (1%)
  local copies, waits for them, and re-layouts  14.3 us (1%)
    psum x1, waiting for transfers between devices, sum_states(): return lax.psum((images_part, variance_part), 'tgt')  541 us
    all_gather x4, waiting for transfers between devices, _take_roads(): u_next = jax.lax.all_gather(z_in, axis)  368 us
  transfers between devices with their start and end apart: 5, of which 5 were waited for; matrix products, arithmetic and copies ran while one was open for 1% of the time, Pallas kernels for 0%

profile of v1, /device:TPU:1, one launch (start us, length us, event | category | flops | bytes accessed | tf_op | source)
XLA Modules:
  0.0 1029.4 jit_solution(7396323300032595711)
XLA Ops:
  7.2 1.4 fusion.412
  11.2 1.6 broadcast_select_fusion.3
  15.0 1.4 broadcast_multiply_fusion.5
  16.5 0.8 slice_bitcast_fusion.22
  17.3 96.4 %all-gather.7.cloned.1.call-done = f32[64,8,3,1024]{3,1,2,0:T(8,128)} async-done(((f32[1,8,3,1024]{3,1,2,0:T(8,128)}), f32[64,8,3,1024]{3,1,2,0:T(8,128)}) %all-gather.7.cloned.1.call-update) | async-done | bytes 6291472 | tf_op jit(solution)/shard_map/all_gather | solution.py:18
  113.7 3.1 reduce_sum.282
  116.9 90.3 %all-gather.11.cloned.1.call-done = f32[64,8,3,1024]{3,1,2,0:T(8,128)} async-done(((f32[1,8,3,1024]{3,1,2,0:T(8,128)}), f32[64,8,3,1024]{3,1,2,0:T(8,128)}) %all-gather.11.cloned.1.call-update) | async-done | bytes 6291472 | tf_op jit(solution)/shard_map/all_gather | solution.py:18
  207.2 3.1 reduce_sum.289
  210.3 90.3 %all-gather.9.cloned.1.call-done = f32[64,8,3,1024]{3,1,2,0:T(8,128)} async-done(((f32[1,8,3,1024]{3,1,2,0:T(8,128)}), f32[64,8,3,1024]{3,1,2,0:T(8,128)}) %all-gather.9.cloned.1.call-update) | async-done | bytes 6291472 | tf_op jit(solution)/shard_map/all_gather | solution.py:18
  300.6 3.1 reduce_sum.287
  303.9 90.6 %all-gather.5.cloned.1.call-done = f32[64,8,3,1024]{3,1,2,0:T(8,128)} async-done(((f32[1,8,3,1024]{3,1,2,0:T(8,128)}), f32[64,8,3,1024]{3,1,2,0:T(8,128)}) %all-gather.5.cloned.1.call-update) | async-done | bytes 6291472 | tf_op jit(solution)/shard_map/all_gather | solution.py:18
  394.5 3.1 reduce_sum.280
  405.3 1.4 fusion.227
  407.1 1.2 add_multiply_fusion.15
  412.5 1.7 add_multiply_fusion.1
  415.3 1.2 add_multiply_fusion.13
  418.3 4.4 add_reduce_fusion
  423.2 14.4 %psum.63 = f32[8,100]{1,0:T(8,128)S(1)} all-reduce(f32[8,100]{1,0:T(8,128)S(1)} %convolution_add_fusion), channel_id=1, replica_groups=mesh['tgt'=64,'sup'=8] {'sup'}, use_global_device_ids=true, to_apply=%region_8.9 | all-reduce | flops 800 | bytes 6400 | tf_op jit(solution)/shard_map/psum | solution.py:106
  437.7 1.0 broadcast_multiply_fusion.13
  438.7 0.9 broadcast_multiply_fusion.12
  439.6 0.9 broadcast_multiply_fusion.11
  440.5 0.9 broadcast_multiply_fusion.14
  441.4 3.0 fusion.206
  447.2 0.9 slice_select_fusion.15
  448.2 0.9 fusion.205
  449.1 0.9 fusion.211
  450.0 0.9 fusion.155
  452.5 0.9 fusion.204
  453.5 1.0 fusion.146
  454.4 0.9 fusion.125
  457.9 0.9 fusion.207
  458.8 1.0 fusion.116
  466.4 540.9 %all-reduce.295.cloned.1.call-done = (f32[8,3,1024]{2,0,1:T(8,128)}, f32[3,8,1024]{2,1,0:T(8,128)}, f32[8,3,1024]{2,0,1:T(8,128)}, f32[3,8,1024]{2,1,0:T(8,128)}...) async-done(((f32[8,3,1024]{2,0,1:T(8,128)}, f32[3,8,1024]{2,1,0:T(8,128)}, f32[8,3,1024]{2,0,1:T(8,128)}, ...) | async-done | bytes 786448 | tf_op jit(solution)/shard_map/psum | solution.py:78
  1007.3 0.8 fusion.240
  1008.2 0.8 fusion.247
  1008.9 0.8 fusion.254
  1009.7 0.8 fusion.261
  1010.8 0.8 pad_add_fusion.47
  1011.6 0.8 pad_add_fusion.44
  1012.5 0.8 fusion.257
  1013.5 0.9 fusion.264
  1014.4 0.8 pad_add_fusion.41
  1015.5 0.8 fusion.250
  1016.6 0.9 fusion.253
  1017.5 0.9 fusion.267
  1018.5 0.9 fusion.260
  1019.4 0.8 pad_add_fusion.38
  1021.8 0.8 pad_maximum_fusion
  (342 shorter events, 33.1 us)
Async XLA Ops:
  7.2 106.6 %all-gather.7.cloned.1.call-start = ((), (), s32[]{:S(2)}) async-start(), calls=%async_computation.1 | async-start | bytes 6389760 | tf_op jit(solution)/shard_map/all_gather | solution.py:18
  12.8 194.3 %all-gather.11.cloned.1.call-start = ((), (), s32[]{:S(2)}) async-start(), calls=%async_computation.3 | async-start | bytes 6389760 | tf_op jit(solution)/shard_map/all_gather | solution.py:18
  13.6 287.0 %all-gather.9.cloned.1.call-start = ((), (), s32[]{:S(2)}) async-start(), calls=%async_computation.2 | async-start | bytes 6389760 | tf_op jit(solution)/shard_map/all_gather | solution.py:18
  14.3 380.2 %all-gather.5.cloned.1.call-start = ((), (), s32[]{:S(2)}) async-start(), calls=%async_computation | async-start | bytes 6389760 | tf_op jit(solution)/shard_map/all_gather | solution.py:18
  14.9 992.4 %all-reduce.295.cloned.1.call-start = ((), (), s32[]{:S(2)}) async-start(), calls=%async_computation.4 | async-start | bytes 1572864 | tf_op jit(solution)/shard_map/psum | solution.py:78
  398.2 5.3 copy-start.30
  398.2 8.9 copy-start.18
  399.1 8.0 copy-start
  399.4 15.8 %copy-start.14 = (f32[8,1024]{1,0:T(8,128)}, f32[8,1024]{1,0:T(8,128)S(1)}, u32[]{:S(2)}) copy-start(f32[8,1024]{1,0:T(8,128)S(1)} %get-tuple-element.405) | copy-start | bytes 98308
  399.7 15.5 %copy-start.2 = (f32[8,1024]{1,0:T(8,128)}, f32[8,1024]{1,0:T(8,128)S(1)}, u32[]{:S(2)}) copy-start(f32[8,1024]{1,0:T(8,128)S(1)} %get-tuple-element.316) | copy-start | bytes 98308
  400.0 7.1 copy-start.16
  400.6 1.9 copy-start.41
  400.8 3.3 copy-start.26
  400.8 4.5 copy-start.8
  401.2 3.2 copy-start.24
  401.2 4.1 copy-start.6
  401.6 13.6 %copy-start.20 = (f32[8,1024]{1,0:T(8,128)}, f32[8,1024]{1,0:T(8,128)S(1)}, u32[]{:S(2)}) copy-start(f32[8,1024]{1,0:T(8,128)S(1)} %get-tuple-element.403) | copy-start | bytes 98308
  402.1 2.4 copy-start.43
  402.4 2.2 copy-start.39
  402.7 9.8 copy-start.10
  402.7 9.8 copy-start.12
  417.4 5.3 copy-start.53
  418.0 4.7 copy-start.32
  418.1 4.8 copy-start.33
  418.1 4.8 copy-start.35
  418.3 4.4 copy-start.22
  418.3 4.6 copy-start.34
  437.7 8.4 copy-start.54
  437.7 7.5 copy-start.4
  437.7 7.5 copy-start.5
  437.7 7.5 copy-start.23
  437.7 7.5 copy-start.36
  458.8 4.6 copy-start.46
  458.8 4.6 copy-start.47
  458.8 4.6 copy-start.48
  460.1 552.4 %copy-start.42 = (f32[8,1024]{1,0:T(8,128)S(1)}, f32[8,1024]{1,0:T(8,128)}, u32[]{:S(2)}) copy-start(f32[8,1024]{1,0:T(8,128)} %copy-done.41) | copy-start | bytes 98308
  460.1 553.4 %copy-start.38 = (f32[8,1024]{1,0:T(8,128)S(1)}, f32[8,1024]{1,0:T(8,128)}, u32[]{:S(2)}) copy-start(f32[8,1024]{1,0:T(8,128)} %copy-done.37) | copy-start | bytes 98308
  460.3 555.2 %copy-start.44 = (f32[8,1024]{1,0:T(8,128)S(1)}, f32[8,1024]{1,0:T(8,128)}, u32[]{:S(2)}) copy-start(f32[8,1024]{1,0:T(8,128)} %copy-done.43) | copy-start | bytes 98308
  460.4 556.2 %copy-start.27 = (f32[8,1024]{1,0:T(8,128)S(1)}, f32[8,1024]{1,0:T(8,128)}, u32[]{:S(2)}) copy-start(f32[8,1024]{1,0:T(8,128)} %copy-done.26) | copy-start | bytes 98308
  460.4 557.1 %copy-start.31 = (f32[8,1024]{1,0:T(8,128)S(1)}, f32[8,1024]{1,0:T(8,128)}, u32[]{:S(2)}) copy-start(f32[8,1024]{1,0:T(8,128)} %copy-done.30) | copy-start | bytes 98308
  460.6 557.9 %copy-start.29 = (f32[8,1024]{1,0:T(8,128)S(1)}, f32[8,1024]{1,0:T(8,128)}, u32[]{:S(2)}) copy-start(f32[8,1024]{1,0:T(8,128)} %copy-done.28) | copy-start | bytes 98308
  460.8 560.1 %copy-start.40 = (f32[8,1024]{1,0:T(8,128)S(1)}, f32[8,1024]{1,0:T(8,128)}, u32[]{:S(2)}) copy-start(f32[8,1024]{1,0:T(8,128)} %copy-done.39) | copy-start | bytes 98308
  462.7 558.5 %copy-start.25 = (f32[8,1024]{1,0:T(8,128)S(1)}, f32[8,1024]{1,0:T(8,128)}, u32[]{:S(2)}) copy-start(f32[8,1024]{1,0:T(8,128)} %copy-done.24) | copy-start | bytes 98308
  1007.3 13.6 %copy-start.45 = (f32[3,8,1024]{2,1,0:T(8,128)S(1)}, f32[3,8,1024]{2,1,0:T(8,128)}, u32[]{:S(2)}) copy-start(f32[3,8,1024]{2,1,0:T(8,128)} %get-tuple-element.39) | copy-start | bytes 294916
  1007.3 14.4 %copy-start.52 = (f32[8,3,1024]{2,0,1:T(8,128)S(1)}, f32[8,3,1024]{2,0,1:T(8,128)}, u32[]{:S(2)}) copy-start(f32[8,3,1024]{2,0,1:T(8,128)} %get-tuple-element.44) | copy-start | bytes 294916
  1007.3 14.4 %copy-start.51 = (f32[8,3,1024]{2,0,1:T(8,128)S(1)}, f32[8,3,1024]{2,0,1:T(8,128)}, u32[]{:S(2)}) copy-start(f32[8,3,1024]{2,0,1:T(8,128)} %get-tuple-element.42) | copy-start | bytes 294916
  1007.3 14.4 %copy-start.50 = (f32[8,3,1024]{2,0,1:T(8,128)S(1)}, f32[8,3,1024]{2,0,1:T(8,128)}, u32[]{:S(2)}) copy-start(f32[8,3,1024]{2,0,1:T(8,128)} %get-tuple-element.40) | copy-start | bytes 294916
  1007.3 14.5 %copy-start.49 = (f32[8,3,1024]{2,0,1:T(8,128)S(1)}, f32[8,3,1024]{2,0,1:T(8,128)}, u32[]{:S(2)}) copy-start(f32[8,3,1024]{2,0,1:T(8,128)} %get-tuple-element.38) | copy-start | bytes 294916
  (12 other events, 18.4 us)
Sparse Core Ops, SparseCore 0:
  13.0 100.7 all-gather.6
  117.1 90.0 all-gather.10
  210.5 90.0 all-gather.8
  304.4 90.0 all-gather.4
  466.5 540.7 all-reduce.294
